TPU v7x, 128 devices: a whole 4x4x4 slice. The times are simulated.
128 devices in a mesh: space: 16 (over x_lo, y, core), tm: 8 (over x_hi, z).
Axes of the slice: x: 4 (x_hi: 2, x_lo: 2; x = x_hi * 2 + x_lo), y: 4, z: 4, core: 2. Of those that a mesh axis runs over, the one named last changes fastest.
Arguments:
- vectors: bfloat16 [8, 2, 3, 96, 8192], P('tm', None, None, None, 'space'), may hold values from -6 to 6
- momenta: int32 [2, 3], replicated, may hold values from -3 to 3
- offsets: int32 [16, 3], replicated, may hold values from 0 to 56, as said below
Outputs:
- elementals: float32 [8, 96, 2, 18432], P(None, 'space')
Inputs may be any that keep to these rules, and one draw needn't show every extreme that they name: `offsets`: each row is the corner of one block of 8 x 8 x 8 sites of the 64^3 lattice: its first two coordinates are multiples of 8, its third a multiple of 8; no two rows name the same block, so the blocks never intersect.
All inputs are finite; a program needn't handle non-finite values.
Results may differ from a plain program's by a relative error of at most 0.0055.
Values may be sent and summed in bfloat16 or wider, within the bound.
No kernel may reach another device: no remote copies, remote signals or barrier semaphores. Data moves between devices by JAX's collectives and lax.ppermute only.
A program may use at most 128 MiB of HBM per device.

v0:
```python
import math
import jax
import jax.numpy as jnp
from jax import lax
from jax.sharding import PartitionSpec as P

LAT = 64
BRICK = 8
BRICK_Z = 8


def local_coords(site):
    return jnp.stack([site // (BRICK * BRICK_Z), site // BRICK_Z % BRICK, site % BRICK_Z])


def phases(momenta, coords):
    product = jnp.sum(momenta[:, :, None] * coords[None, :, :], axis=1)
    angle = (product % LAT).astype(jnp.float32) * (2.0 * math.pi / LAT)
    return jnp.stack([jnp.cos(angle), jnp.sin(angle)], axis=1)


def complex_term(w_real, w_imag, v_real, v_imag):
    return (w_real * v_real - w_imag * v_imag, w_real * v_imag + w_imag * v_real)


def cross_rows(phase, row_vecs, vecs):
    rows_f = row_vecs.astype(jnp.float32)
    cosine = phase[:, 0][:, None, None, :]
    sine = phase[:, 1][:, None, None, :]
    real_w = cosine * rows_f[0][None] - sine * rows_f[1][None]
    imag_w = cosine * rows_f[1][None] + sine * rows_f[0][None]
    real_w = jnp.transpose(real_w, (2, 0, 1, 3))
    imag_w = jnp.transpose(imag_w, (2, 0, 1, 3))
    real_v = vecs[0].astype(jnp.float32)
    imag_v = vecs[1].astype(jnp.float32)
    real_parts = []
    imag_parts = []
    for colour in range(3):
        first = (colour + 1) % 3
        second = (colour + 2) % 3
        plus_re, plus_im = complex_term(
            real_w[:, :, first, None, :],
            imag_w[:, :, first, None, :],
            real_v[second][None, None],
            imag_v[second][None, None],
        )
        minus_re, minus_im = complex_term(
            real_w[:, :, second, None, :],
            imag_w[:, :, second, None, :],
            real_v[first][None, None],
            imag_v[first][None, None],
        )
        real_parts.append(plus_re - minus_re)
        imag_parts.append(plus_im - minus_im)
    stacked = jnp.stack([jnp.stack(real_parts, axis=3), jnp.stack(imag_parts, axis=3)], axis=3)
    return stacked.astype(jnp.bfloat16)


def mixing(vecs):
    real_v = vecs[0]
    imag_v = vecs[1]
    return jnp.stack([jnp.stack([real_v, imag_v], axis=1), jnp.stack([-imag_v, real_v], axis=1)])


def body(vectors, momenta, offsets):
    local = vectors[0]
    nvec = local.shape[2]
    sites = local.shape[3]
    groups = lax.axis_size("space")
    rows = nvec // groups
    width = 2 * nvec * nvec
    moments = momenta.shape[0]
    mine = lax.axis_index("space") * rows
    empty = jnp.zeros((rows, moments, width), jnp.float32)
    vec_piece = lax.all_gather(local.reshape(6 * nvec, sites), "space", axis=1, tiled=True)
    length = vec_piece.shape[1]
    block = math.gcd(length, sites)

    def advance(index, acc):
        vec_block = lax.dynamic_slice_in_dim(vec_piece, index * block, block, 1).reshape(
            2, 3, nvec, block
        )
        site_ids = index * block + jnp.arange(block, dtype=jnp.int32)
        brick_ids = site_ids // sites
        coords = local_coords(site_ids % sites) + jnp.transpose(
            jnp.take(offsets, brick_ids, axis=0)
        )
        phase_block = phases(momenta, coords)
        row_vecs = lax.dynamic_slice_in_dim(vec_block, mine, rows, 2)
        crossed = cross_rows(phase_block, row_vecs, vec_block)
        part = jnp.einsum(
            "imjqcg,qcrkg->imjrk", crossed, mixing(vec_block), preferred_element_type=jnp.float32
        )
        return acc + part.reshape(rows, moments, width)

    summed = lax.fori_loop(0, length // block, advance, empty)
    finished = summed * (1.0 / math.sqrt(sites * groups))
    gathered = lax.all_gather(finished[None], "tm", axis=0, tiled=True)
    return gathered


def solution(mesh):
    return jax.shard_map(
        body,
        mesh=mesh,
        in_specs=(P("tm", None, None, None, "space"), P(), P()),
        out_specs=P(None, "space", None, None),
        check_vma=False,
    )
```

profile of v0, /device:TPU:1, one launch (start us, length us, event | category | flops | bytes accessed | tf_op | source)
XLA Modules:
  0.0 420.6 jit_solution(780666687985766581)
XLA Ops:
  8.8 60.9 %all-gather.4.cloned.1.call-done = bf16[576,8192]{1,0:T(8,128)(2,1)} async-done(((bf16[576,512]{1,0:T(8,128)(2,1)}), bf16[576,8192]{1,0:T(8,128)(2,1)}) %all-gather.4.cloned.1.call-update) | async-done | bytes 9437200 | tf_op jit(solution)/shard_map/all_gather | solution.py:75
  69.7 240.3 %while.17 = (s32[]{:T(128)}, f32[6,2,18432]{2,1,0:T(2,128)S(1)}, s32[2,3]{0,1:T(4,128)S(1)}, s32[16,3]{1,0:T(8,128)S(1)}, bf16[576,8192]{1,0:T(8,128)(2,1)}, /*i...) while((s32[]{:T(128)}, f32[6,2,18432]{2,1,0:T(2,128)S(1)}, ...), condition=%wide.region_2.3_spmd.clone, body=%wide.region_0.2_spmd.clone.sunk | while | flops 1412249600 | bytes 46142696 | solution.py:96
  73.8 4.4 %subtract_convert_fusion.7 = (bf16[6,2,96,1,512]{4,2,3,1,0:T(8,128)(2,1)S(1)}, bf16[6,2,96,1,512]{4,2,3,1,0:T(8,128)(2,1)S(1)}, bf16[6,2,96,1,512]{4,2,3,1,0:T(8...) fusion(f32[96,512]{1,0:T(8,128)S(1)} %get-tuple-element.381, ...), kind=kLoop, calls=%fused_computation.12.clone.1 | loop fusion | flops 28311552 | bytes 8404992 | tf_op jit(solution)/shard_map/convert.7
  79.3 2.0 fusion.24
  82.3 1.6 reshape.462
  88.8 4.4 %subtract_convert_fusion.7 = (bf16[6,2,96,1,512]{4,2,3,1,0:T(8,128)(2,1)S(1)}, bf16[6,2,96,1,512]{4,2,3,1,0:T(8,128)(2,1)S(1)}, bf16[6,2,96,1,512]{4,2,3,1,0:T(8...) fusion(f32[96,512]{1,0:T(8,128)S(1)} %get-tuple-element.381, ...), kind=kLoop, calls=%fused_computation.12.clone.1 | loop fusion | flops 28311552 | bytes 8404992 | tf_op jit(solution)/shard_map/convert.7
  94.3 2.0 fusion.24
  97.3 1.6 reshape.462
  103.8 4.4 %subtract_convert_fusion.7 = (bf16[6,2,96,1,512]{4,2,3,1,0:T(8,128)(2,1)S(1)}, bf16[6,2,96,1,512]{4,2,3,1,0:T(8,128)(2,1)S(1)}, bf16[6,2,96,1,512]{4,2,3,1,0:T(8...) fusion(f32[96,512]{1,0:T(8,128)S(1)} %get-tuple-element.381, ...), kind=kLoop, calls=%fused_computation.12.clone.1 | loop fusion | flops 28311552 | bytes 8404992 | tf_op jit(solution)/shard_map/convert.7
  109.3 2.0 fusion.24
  112.3 1.6 reshape.462
  118.9 4.4 %subtract_convert_fusion.7 = (bf16[6,2,96,1,512]{4,2,3,1,0:T(8,128)(2,1)S(1)}, bf16[6,2,96,1,512]{4,2,3,1,0:T(8,128)(2,1)S(1)}, bf16[6,2,96,1,512]{4,2,3,1,0:T(8...) fusion(f32[96,512]{1,0:T(8,128)S(1)} %get-tuple-element.381, ...), kind=kLoop, calls=%fused_computation.12.clone.1 | loop fusion | flops 28311552 | bytes 8404992 | tf_op jit(solution)/shard_map/convert.7
  124.4 2.0 fusion.24
  127.3 1.6 reshape.462
  133.9 4.4 %subtract_convert_fusion.7 = (bf16[6,2,96,1,512]{4,2,3,1,0:T(8,128)(2,1)S(1)}, bf16[6,2,96,1,512]{4,2,3,1,0:T(8,128)(2,1)S(1)}, bf16[6,2,96,1,512]{4,2,3,1,0:T(8...) fusion(f32[96,512]{1,0:T(8,128)S(1)} %get-tuple-element.381, ...), kind=kLoop, calls=%fused_computation.12.clone.1 | loop fusion | flops 28311552 | bytes 8404992 | tf_op jit(solution)/shard_map/convert.7
  139.4 2.0 fusion.24
  142.3 1.6 reshape.462
  148.9 4.4 %subtract_convert_fusion.7 = (bf16[6,2,96,1,512]{4,2,3,1,0:T(8,128)(2,1)S(1)}, bf16[6,2,96,1,512]{4,2,3,1,0:T(8,128)(2,1)S(1)}, bf16[6,2,96,1,512]{4,2,3,1,0:T(8...) fusion(f32[96,512]{1,0:T(8,128)S(1)} %get-tuple-element.381, ...), kind=kLoop, calls=%fused_computation.12.clone.1 | loop fusion | flops 28311552 | bytes 8404992 | tf_op jit(solution)/shard_map/convert.7
  154.4 2.0 fusion.24
  157.3 1.6 reshape.462
  163.9 4.4 %subtract_convert_fusion.7 = (bf16[6,2,96,1,512]{4,2,3,1,0:T(8,128)(2,1)S(1)}, bf16[6,2,96,1,512]{4,2,3,1,0:T(8,128)(2,1)S(1)}, bf16[6,2,96,1,512]{4,2,3,1,0:T(8...) fusion(f32[96,512]{1,0:T(8,128)S(1)} %get-tuple-element.381, ...), kind=kLoop, calls=%fused_computation.12.clone.1 | loop fusion | flops 28311552 | bytes 8404992 | tf_op jit(solution)/shard_map/convert.7
  169.4 2.0 fusion.24
  178.9 4.4 %subtract_convert_fusion.7 = (bf16[6,2,96,1,512]{4,2,3,1,0:T(8,128)(2,1)S(1)}, bf16[6,2,96,1,512]{4,2,3,1,0:T(8,128)(2,1)S(1)}, bf16[6,2,96,1,512]{4,2,3,1,0:T(8...) fusion(f32[96,512]{1,0:T(8,128)S(1)} %get-tuple-element.381, ...), kind=kLoop, calls=%fused_computation.12.clone.1 | loop fusion | flops 28311552 | bytes 8404992 | tf_op jit(solution)/shard_map/convert.7
  184.4 2.0 fusion.24
  187.4 1.6 reshape.462
  194.0 4.4 %subtract_convert_fusion.7 = (bf16[6,2,96,1,512]{4,2,3,1,0:T(8,128)(2,1)S(1)}, bf16[6,2,96,1,512]{4,2,3,1,0:T(8,128)(2,1)S(1)}, bf16[6,2,96,1,512]{4,2,3,1,0:T(8...) fusion(f32[96,512]{1,0:T(8,128)S(1)} %get-tuple-element.381, ...), kind=kLoop, calls=%fused_computation.12.clone.1 | loop fusion | flops 28311552 | bytes 8404992 | tf_op jit(solution)/shard_map/convert.7
  199.5 2.0 fusion.24
  209.0 4.4 %subtract_convert_fusion.7 = (bf16[6,2,96,1,512]{4,2,3,1,0:T(8,128)(2,1)S(1)}, bf16[6,2,96,1,512]{4,2,3,1,0:T(8,128)(2,1)S(1)}, bf16[6,2,96,1,512]{4,2,3,1,0:T(8...) fusion(f32[96,512]{1,0:T(8,128)S(1)} %get-tuple-element.381, ...), kind=kLoop, calls=%fused_computation.12.clone.1 | loop fusion | flops 28311552 | bytes 8404992 | tf_op jit(solution)/shard_map/convert.7
  214.5 2.0 fusion.24
  217.4 1.6 reshape.462
  224.0 4.4 %subtract_convert_fusion.7 = (bf16[6,2,96,1,512]{4,2,3,1,0:T(8,128)(2,1)S(1)}, bf16[6,2,96,1,512]{4,2,3,1,0:T(8,128)(2,1)S(1)}, bf16[6,2,96,1,512]{4,2,3,1,0:T(8...) fusion(f32[96,512]{1,0:T(8,128)S(1)} %get-tuple-element.381, ...), kind=kLoop, calls=%fused_computation.12.clone.1 | loop fusion | flops 28311552 | bytes 8404992 | tf_op jit(solution)/shard_map/convert.7
  229.5 2.0 fusion.24
  239.0 4.4 %subtract_convert_fusion.7 = (bf16[6,2,96,1,512]{4,2,3,1,0:T(8,128)(2,1)S(1)}, bf16[6,2,96,1,512]{4,2,3,1,0:T(8,128)(2,1)S(1)}, bf16[6,2,96,1,512]{4,2,3,1,0:T(8...) fusion(f32[96,512]{1,0:T(8,128)S(1)} %get-tuple-element.381, ...), kind=kLoop, calls=%fused_computation.12.clone.1 | loop fusion | flops 28311552 | bytes 8404992 | tf_op jit(solution)/shard_map/convert.7
  244.5 2.0 fusion.24
  247.5 1.6 reshape.462
  254.0 4.4 %subtract_convert_fusion.7 = (bf16[6,2,96,1,512]{4,2,3,1,0:T(8,128)(2,1)S(1)}, bf16[6,2,96,1,512]{4,2,3,1,0:T(8,128)(2,1)S(1)}, bf16[6,2,96,1,512]{4,2,3,1,0:T(8...) fusion(f32[96,512]{1,0:T(8,128)S(1)} %get-tuple-element.381, ...), kind=kLoop, calls=%fused_computation.12.clone.1 | loop fusion | flops 28311552 | bytes 8404992 | tf_op jit(solution)/shard_map/convert.7
  259.5 2.0 fusion.24
  262.5 1.6 reshape.462
  269.1 4.4 %subtract_convert_fusion.7 = (bf16[6,2,96,1,512]{4,2,3,1,0:T(8,128)(2,1)S(1)}, bf16[6,2,96,1,512]{4,2,3,1,0:T(8,128)(2,1)S(1)}, bf16[6,2,96,1,512]{4,2,3,1,0:T(8...) fusion(f32[96,512]{1,0:T(8,128)S(1)} %get-tuple-element.381, ...), kind=kLoop, calls=%fused_computation.12.clone.1 | loop fusion | flops 28311552 | bytes 8404992 | tf_op jit(solution)/shard_map/convert.7
  274.6 2.0 fusion.24
  277.5 1.6 reshape.462
  284.1 4.4 %subtract_convert_fusion.7 = (bf16[6,2,96,1,512]{4,2,3,1,0:T(8,128)(2,1)S(1)}, bf16[6,2,96,1,512]{4,2,3,1,0:T(8,128)(2,1)S(1)}, bf16[6,2,96,1,512]{4,2,3,1,0:T(8...) fusion(f32[96,512]{1,0:T(8,128)S(1)} %get-tuple-element.381, ...), kind=kLoop, calls=%fused_computation.12.clone.1 | loop fusion | flops 28311552 | bytes 8404992 | tf_op jit(solution)/shard_map/convert.7
  289.6 2.0 fusion.24
  292.5 1.6 reshape.462
  299.1 4.4 %subtract_convert_fusion.7 = (bf16[6,2,96,1,512]{4,2,3,1,0:T(8,128)(2,1)S(1)}, bf16[6,2,96,1,512]{4,2,3,1,0:T(8,128)(2,1)S(1)}, bf16[6,2,96,1,512]{4,2,3,1,0:T(8...) fusion(f32[96,512]{1,0:T(8,128)S(1)} %get-tuple-element.381, ...), kind=kLoop, calls=%fused_computation.12.clone.1 | loop fusion | flops 28311552 | bytes 8404992 | tf_op jit(solution)/shard_map/convert.7
  304.6 2.0 fusion.24
  311.4 95.9 %all-gather.6.cloned.1.call-done = f32[48,2,18432]{2,1,0:T(2,128)} async-done(((f32[6,2,18432]{2,1,0:T(2,128)}), f32[48,2,18432]{2,1,0:T(2,128)}) %all-gather.6.cloned.1.call-update) | async-done | bytes 7077904 | tf_op jit(solution)/shard_map/all_gather | solution.py:98
  407.3 6.4 %copy.46 = f32[8,6,2,18432]{3,2,1,0:T(2,128)} copy(f32[8,6,2,18432]{3,2,1,0:T(2,128)} %bitcast.88) | data formatting | bytes 14155776
  (412 shorter events, 118.4 us)
Async XLA Ops:
  6.5 63.2 %all-gather.4.cloned.1.call-start = ((), (), s32[]{:S(2)}) async-start(), calls=%async_computation | async-start | bytes 10027008 | tf_op jit(solution)/shard_map/all_gather | solution.py:75
  7.3 400.1 %all-gather.6.cloned.1.call-start = ((), (), s32[]{:S(2)}) async-start(), calls=%async_computation.1 | async-start | bytes 7962624 | tf_op jit(solution)/shard_map/all_gather | solution.py:98
Sparse Core Ops, SparseCore 0:
  9.0 60.6 all-gather.3
  311.5 95.7 all-gather.5
where the time goes:
time: 422 us; the launch traced here: 421 us
  waiting for transfers between devices  158 us (37%)
  other arithmetic  109 us (26%)
  local copies, waits for them, and re-layouts  105 us (25%)
  matrix products  32.4 us (8%)
  between operations  13.4 us (3%)
    all_gather x1, waiting for transfers between devices, body(): gathered = lax.all_gather(finished[None], 'tm', axis=0, tiled=True)  95.9 us
    another operation x16, other arithmetic  71.1 us
    all_gather x1, waiting for transfers between devices, body(): lax.all_gather(local.reshape(6 * nvec, sites), 'space', axis=1, tiled=True)  60.9 us
    dot_general x16, matrix products, advance(): jnp.einsum('imjqcg,qcrkg->imjrk', crossed, mixing(vec_block), preferred_e...  32.4 us
    reshape x16, local copies, waits for them, and re-layouts, advance(): return acc + part.reshape(rows, moments, width)  25.2 us
    gather x32, local copies, waits for them, and re-layouts, advance(): jnp.take(offsets, brick_ids, axis=0)  18.3 us
    dynamic_slice x16, local copies, waits for them, and re-layouts, advance(): lax.dynamic_slice_in_dim(vec_piece, index * block, block, 1)  17.7 us
    slice x16, local copies, waits for them, and re-layouts, cross_rows(): real_v = vecs[0].astype(jnp.float32)  17.6 us
  transfers between devices with their start and end apart: 2, of which 2 were waited for; matrix products, arithmetic and copies ran while one was open for 0% of the time, Pallas kernels for 0%

commit v1 on v0

--- a/solution.py
+++ b/solution.py
@@ -7,6 +7,13 @@
 LAT = 64
 BRICK = 8
 BRICK_Z = 8
+
+
+def find_flows(arr):
+    known = jax.lax.psum(1, "space")
+    view_out = jnp.stack([arr] * known)
+    even = jax.lax.all_to_all(view_out, axis_name="space", split_axis=0, concat_axis=0)
+    return jnp.concatenate(even, axis=1)
 
 
 def local_coords(site):
@@ -72,7 +79,7 @@
     moments = momenta.shape[0]
     mine = lax.axis_index("space") * rows
     empty = jnp.zeros((rows, moments, width), jnp.float32)
-    vec_piece = lax.all_gather(local.reshape(6 * nvec, sites), "space", axis=1, tiled=True)
+    vec_piece = find_flows(local.reshape(6 * nvec, sites))
     length = vec_piece.shape[1]
     block = math.gcd(length, sites)
 

time: 422 us -> 526 us (1.25)
  waiting for transfers between devices: 158 us -> 242 us
  local copies, waits for them, and re-layouts: 105 us -> 118 us
  starting transfers between devices: 0.04 us -> 7.08 us
    all_to_all x0 -> x1, waiting for transfers between devices: none -> 139 us  [find_flows(): jax.lax.all_to_all(view_out, axis_name='space', split_axis=0, concat_axis=0)]
    all_gather x1 -> x0, waiting for transfers between devices: 60.9 us -> none  [body(): lax.all_gather(local.reshape(6 * nvec, sites), 'space', axis=1, tiled=True)]
    reshape x0 -> x1, local copies, waits for them, and re-layouts: none -> 8.74 us  [find_flows(): return jnp.concatenate(even, axis=1)]
    all_to_all x0 -> x1, starting transfers between devices: none -> 7.05 us  [find_flows(): jax.lax.all_to_all(view_out, axis_name='space', split_axis=0, concat_axis=0)]
    all_gather x1, waiting for transfers between devices: 95.9 us -> 103 us  [body(): gathered = lax.all_gather(finished[None], 'tm', axis=0, tiled=True)]
    another operation x0 -> x1, local copies, waits for them, and re-layouts: none -> 5.63 us  [find_flows(): view_out = jnp.stack([arr] * known)]
where the time goes in v1:
time: 526 us; the launch traced here: 525 us
  waiting for transfers between devices  242 us (46%)
  local copies, waits for them, and re-layouts  118 us (22%)
  other arithmetic  109 us (21%)
  matrix products  32.4 us (6%)
  between operations  13.4 us (3%)
  starting transfers between devices  7.08 us (1%)
    all_to_all x1, waiting for transfers between devices, find_flows(): jax.lax.all_to_all(view_out, axis_name='space', split_axis=0, concat_axis=0)  139 us
    all_gather x1, waiting for transfers between devices, body(): gathered = lax.all_gather(finished[None], 'tm', axis=0, tiled=True)  103 us
    another operation x16, other arithmetic  71.1 us
    dot_general x16, matrix products, advance(): jnp.einsum('imjqcg,qcrkg->imjrk', crossed, mixing(vec_block), preferred_e...  32.4 us
    reshape x16, local copies, waits for them, and re-layouts, advance(): return acc + part.reshape(rows, moments, width)  25.2 us
    gather x32, local copies, waits for them, and re-layouts, advance(): jnp.take(offsets, brick_ids, axis=0)  18.3 us
    dynamic_slice x16, local copies, waits for them, and re-layouts, advance(): lax.dynamic_slice_in_dim(vec_piece, index * block, block, 1)  17.7 us
    slice x16, local copies, waits for them, and re-layouts, cross_rows(): real_v = vecs[0].astype(jnp.float32)  17.6 us
  transfers between devices with their start and end apart: 2, of which 2 were waited for; matrix products, arithmetic and copies ran while one was open for 0% of the time, Pallas kernels for 0%

profile of v1, /device:TPU:1, one launch (start us, length us, event | category | flops | bytes accessed | tf_op | source)
XLA Modules:
  0.0 524.8 jit_solution(6195186597421942202)
XLA Ops:
  6.5 5.6 %stack.165 = bf16[16,576,512]{2,1,0:T(8,128)(2,1)} broadcast(bf16[576,512]{1,0:T(8,128)(2,1)} %bitcast.93), dimensions={1,2} | broadcast | bytes 10027008 | tf_op jit(solution)/shard_map/stack | solution.py:14
  12.2 7.0 %all-to-all-start = ((bf16[16,576,512]{2,1,0:T(8,128)(2,1)}), bf16[16,576,512]{2,1,0:T(8,128)(2,1)}, u32[]{:S(2)}, u32[]{:S(2)}) async-start(bf16[16,576,512]{2,1,0:T(8,128)(2,1)} %stack.165), calls=%async_computation | async-start | bytes 18874368 | tf_op jit(solution)/shard_map/all_to_all | solution.py:15
  19.5 139.1 %all-to-all-done = bf16[16,576,512]{2,1,0:T(8,128)(2,1)} async-done(((bf16[16,576,512]{2,1,0:T(8,128)(2,1)}), bf16[16,576,512]{2,1,0:T(8,128)(2,1)}, u32[]{:S(2)}, u32[]{:S(2)}) %all-to-all-start) | async-done | bytes 9437216 | tf_op jit(solution)/shard_map/all_to_all | solution.py:15
  158.6 8.7 %copy.44 = bf16[16,72,8,512]{3,2,0,1:T(8,128)(2,1)} copy(bf16[16,72,8,512]{3,2,1,0:T(8,128)(2,1)} %bitcast.37) | data formatting | bytes 18874368 | tf_op jit(solution)/shard_map/reshape | solution.py:16
  167.3 240.3 %while.17 = (s32[]{:T(128)}, f32[6,2,18432]{2,1,0:T(2,128)S(1)}, s32[2,3]{0,1:T(4,128)S(1)}, s32[16,3]{1,0:T(8,128)S(1)}, bf16[576,8192]{1,0:T(8,128)(2,1)}, /*i...) while((s32[]{:T(128)}, f32[6,2,18432]{2,1,0:T(2,128)S(1)}, ...), condition=%wide.region_2.3_spmd.clone, body=%wide.region_0.2_spmd.clone.sunk | while | flops 1412249600 | bytes 46142696 | solution.py:103
  171.4 4.4 subtract_convert_fusion.7
  176.9 2.0 fusion.24
  179.9 1.6 reshape.472
  186.4 4.4 subtract_convert_fusion.7
  191.9 2.0 fusion.24
  194.9 1.6 reshape.472
  201.4 4.4 subtract_convert_fusion.7
  206.9 2.0 fusion.24
  209.9 1.6 reshape.472
  216.5 4.4 subtract_convert_fusion.7
  222.0 2.0 fusion.24
  224.9 1.6 reshape.472
  231.5 4.4 subtract_convert_fusion.7
  237.0 2.0 fusion.24
  239.9 1.6 reshape.472
  246.5 4.4 subtract_convert_fusion.7
  252.0 2.0 fusion.24
  255.0 1.6 reshape.472
  261.5 4.4 subtract_convert_fusion.7
  267.0 2.0 fusion.24
  270.0 1.6 reshape.472
  276.5 4.4 subtract_convert_fusion.7
  282.0 2.0 fusion.24
  291.6 4.4 subtract_convert_fusion.7
  297.1 2.0 fusion.24
  300.0 1.6 reshape.472
  306.6 4.4 subtract_convert_fusion.7
  312.1 2.0 fusion.24
  321.6 4.4 subtract_convert_fusion.7
  327.1 2.0 fusion.24
  330.1 1.6 reshape.472
  336.6 4.4 subtract_convert_fusion.7
  342.1 2.0 fusion.24
  351.6 4.4 subtract_convert_fusion.7
  357.1 2.0 fusion.24
  366.7 4.4 subtract_convert_fusion.7
  372.2 2.0 fusion.24
  381.7 4.4 subtract_convert_fusion.7
  387.2 2.0 fusion.24
  396.7 4.4 subtract_convert_fusion.7
  402.2 2.0 fusion.24
  409.0 102.5 %all-gather.3.cloned.1.call-done = f32[48,2,18432]{2,1,0:T(2,128)} async-done(((f32[6,2,18432]{2,1,0:T(2,128)}), f32[48,2,18432]{2,1,0:T(2,128)}) %all-gather.3.cloned.1.call-update) | async-done | bytes 7077904 | tf_op jit(solution)/shard_map/all_gather | solution.py:105
  511.5 6.4 %copy.56 = f32[8,6,2,18432]{3,2,1,0:T(2,128)} copy(f32[8,6,2,18432]{3,2,1,0:T(2,128)} %bitcast.92) | data formatting | bytes 14155776
  (417 shorter events, 121.0 us)
Async XLA Ops:
  12.2 7.1 %copy-start = (s32[16,3]{0,1:T(4,128)S(1)}, s32[16,3]{0,1:T(4,128)}, u32[]{:S(2)}) copy-start(s32[16,3]{0,1:T(4,128)} %param.7) | copy-start | bytes 580
  12.2 7.2 %copy-start.1 = (s32[2,3]{1,0:T(2,128)S(1)}, s32[2,3]{1,0:T(2,128)}, u32[]{:S(2)}) copy-start(s32[2,3]{1,0:T(2,128)} %param.6) | copy-start | bytes 76
  12.2 146.4 %all-to-all-start = ((bf16[16,576,512]{2,1,0:T(8,128)(2,1)}), bf16[16,576,512]{2,1,0:T(8,128)(2,1)}, u32[]{:S(2)}, u32[]{:S(2)}) async-start(bf16[16,576,512]{2,1,0:T(8,128)(2,1)} %stack.165), calls=%async_computation | async-start | bytes 18874368 | tf_op jit(solution)/shard_map/all_to_all | solution.py:15
  19.2 492.3 %all-gather.3.cloned.1.call-start = ((), (), s32[]{:S(2)}) async-start(), calls=%async_computation.1 | async-start | bytes 7962624 | tf_op jit(solution)/shard_map/all_gather | solution.py:105
Sparse Core Ops, SparseCore 0:
  409.1 102.3 all-gather.2
